TPU v7x, 32 devices: a whole 2x2x4 slice. The times are simulated.
32 devices in a mesh: req: 2 (over x), hst: 16 (over z, y, core).
Axes of the slice: x: 2, y: 2, z: 4, core: 2. Of those that a mesh axis runs over, the one named last changes fastest.
Arguments:
- ctx_q: bfloat16 [4096, 4096], P(('req', 'hst')), parts along dimension 0, may hold values from -24 to 24
- ctx_k: bfloat16 [4096, 512], P(('req', 'hst')), parts along dimension 0, may hold values from -8 to 8
- ctx_v: bfloat16 [4096, 512], P(('req', 'hst')), parts along dimension 0, may hold values from -6 to 6
- ask_q: bfloat16 [64, 4096], P(('req', 'hst')), parts along dimension 0, may hold values from -24 to 24
- ask_k: bfloat16 [64, 512], P(('req', 'hst')), parts along dimension 0, may hold values from -9 to 9
- ask_v: bfloat16 [64, 512], P(('req', 'hst')), parts along dimension 0, may hold values from -6 to 6
- valid: int32 [32], P(('req', 'hst')), parts along dimension 0, may hold values from 64 to 128, as said below
Outputs:
- ctx_out: bfloat16 [4096, 4096], P(('req', 'hst')), parts along dimension 0
- ask_out: bfloat16 [64, 4096], P(('req', 'hst')), parts along dimension 0
There are 2 independent parts, one for each index of `req`. A program takes and returns all parts, laid end to end along the dimension named above; each array names one. Nothing has to cross between parts.
Inputs may be any that keep to these rules, and one draw needn't show every extreme that they name: `valid`: block 0, the anchor, is always full.
All inputs are finite; a program needn't handle non-finite values.
Results may differ from a plain program's by a relative error of at most 0.0029.
Values may be sent and summed in bfloat16 or wider, within the bound.
A program may use at most 320 MiB of HBM per device.

v0:
```python
import math

import jax
import jax.numpy as jnp
from jax import lax
from jax.sharding import PartitionSpec as P

H = 32
KVH = 4
DH = 128


def from_root(array, axis, root):
    mine = lax.axis_index(axis) == root
    return lax.psum(jnp.where(mine, array, jnp.zeros_like(array)), axis)


def partial_attend(queries, key_rows, value_rows, visible):
    row_count = queries.shape[0]
    group_size = H // KVH
    group_width = group_size * DH
    scale = 1.0 / math.sqrt(DH)

    def one_group(group_index, carry):
        maxima, totals, outputs = carry
        query_part = lax.dynamic_slice_in_dim(queries, group_index * group_width, group_width, 1)
        query_part = query_part.reshape(row_count, group_size, DH)
        key_part = lax.dynamic_slice_in_dim(key_rows, group_index * DH, DH, 1)
        value_part = lax.dynamic_slice_in_dim(value_rows, group_index * DH, DH, 1)
        scores = (
            jnp.einsum("rgd,sd->rgs", query_part, key_part, preferred_element_type=jnp.float32)
            * scale
        )
        scores = jnp.where(visible[:, None, :], scores, -jnp.inf)
        row_max = jnp.max(scores, axis=-1)
        expon = jnp.exp(scores - row_max[..., None])
        row_sum = jnp.sum(expon, axis=-1)
        weights = expon.astype(jnp.bfloat16)
        mixed = jnp.einsum("rgs,sd->rgd", weights, value_part, preferred_element_type=jnp.float32)
        maxima = lax.dynamic_update_slice_in_dim(maxima, row_max, group_index * group_size, 1)
        totals = lax.dynamic_update_slice_in_dim(totals, row_sum, group_index * group_size, 1)
        outputs = lax.dynamic_update_slice_in_dim(
            outputs, mixed.reshape(row_count, group_width), group_index * group_width, 1
        )
        return (maxima, totals, outputs)

    start_carry = (
        jnp.zeros((row_count, H), jnp.float32),
        jnp.zeros((row_count, H), jnp.float32),
        jnp.zeros((row_count, H * DH), jnp.float32),
    )
    return lax.fori_loop(0, KVH, one_group, start_carry)


def weigh(values, factor):
    shape = values.shape
    return (values.reshape(shape[:-1] + (H, DH)) * factor[..., None]).reshape(shape)


def body(ctx_q, ctx_k, ctx_v, ask_q, ask_k, ask_v, valid):
    block_rows = ctx_q.shape[0]
    host_index = lax.axis_index("hst")
    host_count = lax.axis_size("hst")
    valid_count = valid[0]
    local = jnp.arange(block_rows, dtype=jnp.int32)
    anchor_k, anchor_v = (from_root(ctx_k, "hst", 0), from_root(ctx_v, "hst", 0))
    own_visible = (local[None, :] <= local[:, None]) & (local[None, :] < valid_count)
    anchor_visible = jnp.broadcast_to(host_index > 0, (block_rows, block_rows))
    visible = jnp.concatenate([anchor_visible, own_visible], axis=1)
    row_max, row_sum, mixed = partial_attend(
        ctx_q, jnp.concatenate([anchor_k, ctx_k], 0), jnp.concatenate([anchor_v, ctx_v], 0), visible
    )
    normed = weigh(mixed, 1.0 / row_sum)
    ctx_out = jnp.where(local[:, None] < valid_count, normed, 0.0).astype(jnp.bfloat16)
    all_q, all_k, all_v = (
        lax.all_gather(ask_q, "hst", axis=0, tiled=True),
        lax.all_gather(ask_k, "hst", axis=0, tiled=True),
        lax.all_gather(ask_v, "hst", axis=0, tiled=True),
    )
    query_count = all_q.shape[0]
    query_pos = jnp.arange(query_count, dtype=jnp.int32)
    is_last = host_index == host_count - 1
    ask_visible = jnp.concatenate(
        [
            jnp.broadcast_to(local[None, :] < valid_count, (query_count, block_rows)),
            (query_pos[None, :] <= query_pos[:, None]) & is_last,
        ],
        axis=1,
    )
    ask_max, ask_sum, ask_mixed = partial_attend(
        all_q, jnp.concatenate([ctx_k, all_k], 0), jnp.concatenate([ctx_v, all_v], 0), ask_visible
    )
    maxima, totals, outputs = (
        lax.all_to_all(ask_max[None], "hst", split_axis=1, concat_axis=0, tiled=True),
        lax.all_to_all(ask_sum[None], "hst", split_axis=1, concat_axis=0, tiled=True),
        lax.all_to_all(ask_mixed[None], "hst", split_axis=1, concat_axis=0, tiled=True),
    )
    best = jnp.max(maxima, axis=0)
    scaling = jnp.exp(maxima - best[None])
    total = jnp.sum(totals * scaling, axis=0)
    summed = jnp.sum(weigh(outputs, scaling), axis=0)
    ask_out = weigh(summed, 1.0 / total).astype(jnp.bfloat16)
    return (ctx_out, ask_out)


def solution(mesh):
    in_specs = (
        P(("req", "hst"), None),
        P(("req", "hst"), None),
        P(("req", "hst"), None),
        P(("req", "hst"), None),
        P(("req", "hst"), None),
        P(("req", "hst"), None),
        P(("req", "hst")),
    )
    out_specs = (P(("req", "hst"), None), P(("req", "hst"), None))
    return jax.shard_map(body, mesh=mesh, in_specs=in_specs, out_specs=out_specs, check_vma=False)
```

profile of v0, /device:TPU:9, one launch (start us, length us, event | category | flops | bytes accessed | tf_op | source)
XLA Modules:
  0.0 218.5 jit_solution(2751996907084913244)
XLA Ops:
  7.8 20.3 %all-gather = bf16[16,2,4096]{2,1,0:T(2,128)(2,1)S(1)} all-gather(bf16[1,2,4096]{2,1,0:T(2,128)(2,1)} %bitcast.83), channel_id=1, replica_groups=mesh['req'=2,'hst'=16] {'hst'}, dimensions={0}, use_global_device_ids=true | all-gather | bytes 278528 | tf_op jit(solution)/shard_map/all_gather | solution.py:76
  28.3 17.8 %all-gather.1 = bf16[16,2,512]{2,1,0:T(2,128)(2,1)S(1)} all-gather(bf16[1,2,512]{2,1,0:T(2,128)(2,1)} %bitcast.84), channel_id=1, replica_groups=mesh['req'=2,'hst'=16] {'hst'}, dimensions={0}, use_global_device_ids=true | all-gather | bytes 34816 | tf_op jit(solution)/shard_map/all_gather | solution.py:77
  46.0 19.1 %all-gather.2 = bf16[16,2,512]{2,1,0:T(2,128)(2,1)S(1)} all-gather(bf16[1,2,512]{2,1,0:T(2,128)(2,1)} %bitcast.85), channel_id=1, replica_groups=mesh['req'=2,'hst'=16] {'hst'}, dimensions={0}, use_global_device_ids=true | all-gather | bytes 34816 | tf_op jit(solution)/shard_map/all_gather | solution.py:78
  65.2 0.9 pad_maximum_fusion.2
  66.1 0.9 pad_maximum_fusion.3
  67.0 0.6 broadcast.56
  67.6 0.6 broadcast.56.clone
  68.3 14.5 %while.33 = (s32[]{:T(128)}, f32[32,32]{1,0:T(8,128)}, f32[32,32]{1,0:T(8,128)}, f32[32,4096]{1,0:T(8,128)S(1)}, pred[32,160]{1,0:T(8,128)(4,1)S(1)}, /*index=5*...) while((s32[]{:T(128)}, f32[32,32]{1,0:T(8,128)}, ...), condition=%wide.region_9.10_spmd, body=%wide.region_6.9_spmd.sunk | while | flops 21257740 | bytes 1424703 | solution.py:52
  68.6 1.3 dynamic_update_slice.46
  70.2 1.3 dynamic_update_slice.47
  72.2 1.4 dynamic_update_slice.46
  73.8 1.4 dynamic_update_slice.47
  75.8 1.4 dynamic_update_slice.46
  77.4 1.4 dynamic_update_slice.47
  79.5 1.4 dynamic_update_slice.46
  81.1 1.4 dynamic_update_slice.47
  82.8 6.4 %all-to-all-start.1 = ((f32[1,32,32]{2,0,1:T(1,128)}), f32[1,32,32]{2,0,1:T(1,128)S(1)}, u32[]{:S(2)}, u32[]{:S(2)}) async-start(f32[1,32,32]{2,0,1:T(1,128)} %bitcast.10), calls=%async_computation.1 | async-start | bytes 32768 | tf_op jit(solution)/shard_map/all_to_all | solution.py:94
  89.5 0.7 broadcast_select_fusion
  90.2 4.0 %all-to-all-done.1 = f32[1,32,32]{2,0,1:T(1,128)S(1)} async-done(((f32[1,32,32]{2,0,1:T(1,128)}), f32[1,32,32]{2,0,1:T(1,128)S(1)}, u32[]{:S(2)}, u32[]{:S(2)}) %all-to-all-start.1) | async-done | bytes 4128 | tf_op jit(solution)/shard_map/all_to_all | solution.py:94
  94.3 4.9 %all-to-all-start.2 = ((f32[1,32,32]{2,0,1:T(1,128)}), f32[1,32,32]{2,0,1:T(1,128)S(1)}, u32[]{:S(2)}, u32[]{:S(2)}) async-start(f32[1,32,32]{2,0,1:T(1,128)} %bitcast.12), calls=%async_computation.2 | async-start | bytes 32768 | tf_op jit(solution)/shard_map/all_to_all | solution.py:95
  99.2 1.4 broadcast_in_dim.110
  100.6 3.6 %all-to-all-done.2 = f32[1,32,32]{2,0,1:T(1,128)S(1)} async-done(((f32[1,32,32]{2,0,1:T(1,128)}), f32[1,32,32]{2,0,1:T(1,128)S(1)}, u32[]{:S(2)}, u32[]{:S(2)}) %all-to-all-start.2) | async-done | bytes 4128 | tf_op jit(solution)/shard_map/all_to_all | solution.py:95
  104.2 5.0 %all-to-all-start = ((f32[1,32,4096]{2,0,1:T(1,128)}), f32[1,32,4096]{2,0,1:T(1,128)S(1)}, u32[]{:S(2)}, u32[]{:S(2)}) async-start(f32[1,32,4096]{2,0,1:T(1,128)} %broadcast_in_dim.110), calls=%async_computation | async-start | bytes 1048576 | tf_op jit(solution)/shard_map/all_to_all | solution.py:96
  109.8 77.9 %all-reduce.4.cloned.1.call-done = (bf16[128,512]{0,1:T(8,128)(2,1)}, bf16[128,512]{0,1:T(8,128)(2,1)}) async-done(((bf16[128,512]{0,1:T(8,128)(2,1)}, bf16[128,512]{0,1:T(8,128)(2,1)}), (bf16[128,512]{0,1:T(8,128)(2,1)}, bf16[128,512]{0,1:T(8,128)(2,1)})) %all-reduce.4.cloned.1.call-update) | async-done | bytes 262160 | tf_op jit(solution)/shard_map/psum | solution.py:15
  187.7 0.9 pad_maximum_fusion
  188.7 0.9 pad_maximum_fusion.1
  189.6 1.6 broadcast_in_dim.107.clone2
  191.2 13.8 %while.32 = (s32[]{:T(128)}, f32[128,32]{0,1:T(8,128)S(1)}, f32[128,4096]{1,0:T(8,128)}, pred[128,256]{1,0:T(8,128)(4,1)S(1)}, bf16[128,4096]{1,0:T(8,128)(2,1)}...) while((s32[]{:T(128)}, f32[128,32]{0,1:T(8,128)S(1)}, ...), condition=%wide.region_5.6_spmd, body=%wide.region_2.5_spmd.sunk | while | flops 136050688 | bytes 7266611 | solution.py:52
  191.2 1.0 constant_dynamic-slice_fusion.2
  192.3 0.4 fusion.48
  193.2 0.4 fusion.50
  193.8 0.8 constant_dynamic-update-slice_fusion.5
  194.6 1.0 constant_dynamic-slice_fusion.2
  195.8 0.4 fusion.48
  196.6 0.4 fusion.50
  197.2 0.9 constant_dynamic-update-slice_fusion.5
  198.1 1.0 constant_dynamic-slice_fusion.2
  199.2 0.4 fusion.48
  200.1 0.4 fusion.50
  200.7 0.8 constant_dynamic-update-slice_fusion.5
  201.5 1.0 constant_dynamic-slice_fusion.2
  202.7 0.4 fusion.48
  204.1 0.9 constant_dynamic-update-slice_fusion.5
  205.1 0.6 mul.103
  205.7 0.9 copy-done
  206.6 2.6 %fusion.25 = bf16[128,4096]{1,0:T(8,128)(2,1)} fusion(f32[128,4096]{1,0:T(8,128)S(1)} %copy-done, f32[16,8,32,128]{3,2,1,0:T(8,128)S(1)} %bitcast.78, pred[128]{0:T(512)(128)(4,1)S(1)} %iota_compare_fusion.2), kind=kLoop, calls=%fused_computation.33 | loop fusion | flops 1572864 | bytes 5243008 | tf_op jit(solution)/shard_map/convert_element_type | solution.py:74
  209.1 1.2 reduce
  211.0 0.6 fusion.27
  (72 shorter events, 8.3 us)
Async XLA Ops:
  68.2 21.0 %copy-start.1 = (bf16[128,512]{1,0:T(8,128)(2,1)S(1)}, bf16[128,512]{1,0:T(8,128)(2,1)}, u32[]{:S(2)}) copy-start(bf16[128,512]{1,0:T(8,128)(2,1)} %param.12) | copy-start | bytes 393220
  68.3 21.1 %copy-start.2 = (bf16[128,512]{1,0:T(8,128)(2,1)S(1)}, bf16[128,512]{1,0:T(8,128)(2,1)}, u32[]{:S(2)}) copy-start(bf16[128,512]{1,0:T(8,128)(2,1)} %param.13) | copy-start | bytes 393220
  82.8 11.4 %all-to-all-start.1 = ((f32[1,32,32]{2,0,1:T(1,128)}), f32[1,32,32]{2,0,1:T(1,128)S(1)}, u32[]{:S(2)}, u32[]{:S(2)}) async-start(f32[1,32,32]{2,0,1:T(1,128)} %bitcast.10), calls=%async_computation.1 | async-start | bytes 32768 | tf_op jit(solution)/shard_map/all_to_all | solution.py:94
  89.2 98.5 %all-reduce.4.cloned.1.call-start = ((), (), s32[]{:S(2)}) async-start(), calls=%async_computation.3 | async-start | bytes 524288 | tf_op jit(solution)/shard_map/psum | solution.py:15
  94.3 10.0 %all-to-all-start.2 = ((f32[1,32,32]{2,0,1:T(1,128)}), f32[1,32,32]{2,0,1:T(1,128)S(1)}, u32[]{:S(2)}, u32[]{:S(2)}) async-start(f32[1,32,32]{2,0,1:T(1,128)} %bitcast.12), calls=%async_computation.2 | async-start | bytes 32768 | tf_op jit(solution)/shard_map/all_to_all | solution.py:95
  104.2 104.9 %all-to-all-start = ((f32[1,32,4096]{2,0,1:T(1,128)}), f32[1,32,4096]{2,0,1:T(1,128)S(1)}, u32[]{:S(2)}, u32[]{:S(2)}) async-start(f32[1,32,4096]{2,0,1:T(1,128)} %broadcast_in_dim.110), calls=%async_computation | async-start | bytes 1048576 | tf_op jit(solution)/shard_map/all_to_all | solution.py:96
  205.0 1.6 copy-start
Sparse Core Ops, SparseCore 0:
  94.0 93.6 all-reduce.3
where the time goes:
time: 222 us; the launch traced here: 218 us
  waiting for transfers between devices  85.5 us (39%)
  blocking collectives  57.1 us (26%)
  local copies, waits for them, and re-layouts  27.2 us (12%)
  starting transfers between devices  16.3 us (7%)
  between operations  14.9 us (7%)
  other arithmetic  11.6 us (5%)
  matrix products  5.35 us (2%)
    psum x1, waiting for transfers between devices, from_root(): return lax.psum(jnp.where(mine, array, jnp.zeros_like(array)), axis)  77.9 us
    all_gather x1, blocking collectives, body(): lax.all_gather(ask_q, 'hst', axis=0, tiled=True)  20.3 us
    all_gather x1, blocking collectives, body(): lax.all_gather(ask_v, 'hst', axis=0, tiled=True)  19.1 us
    all_gather x1, blocking collectives, body(): lax.all_gather(ask_k, 'hst', axis=0, tiled=True)  17.8 us
    all_to_all x1, starting transfers between devices, body(): lax.all_to_all(ask_max[None], 'hst', split_axis=1, concat_axis=0, tiled=T...  6.36 us
    dynamic_update_slice x8, local copies, waits for them, and re-layouts, one_group(): lax.dynamic_update_slice_in_dim(totals, row_sum, group_index * group_size...  5.62 us
    dynamic_update_slice x4, local copies, waits for them, and re-layouts, one_group(): lax.dynamic_update_slice_in_dim(maxima, row_max, group_index * group_size...  5.61 us
    all_to_all x1, starting transfers between devices, body(): lax.all_to_all(ask_mixed[None], 'hst', split_axis=1, concat_axis=0, tiled...  5.03 us
  transfers between devices with their start and end apart: 4, of which 3 were waited for; matrix products, arithmetic and copies ran while one was open for 11% of the time, Pallas kernels for 0%

commit v1 on v0

v1 whole, which is shorter than its diff:
```python
import functools
import math

import jax
import jax.numpy as jnp
from jax import lax
from jax.experimental import pallas as pl
from jax.experimental.pallas import tpu as pltpu
from jax.sharding import PartitionSpec as P

H = 32
KVH = 4
DH = 128
G = H // KVH
C = math.log2(math.e) / math.sqrt(DH)
NT = (((1,), (1,)), ((), ()))
NN = (((1,), (0,)), ((), ()))


def remote(src, dst, send_sem, recv_sem, target):
    return pltpu.make_async_remote_copy(
        src_ref=src,
        dst_ref=dst,
        send_sem=send_sem,
        recv_sem=recv_sem,
        device_id={"hst": target},
        device_id_type=pl.DeviceIdType.MESH,
    )


def kernel(
    n, ctx_q, ctx_k, ctx_v, pack, ctx_out, ask_out,
    qbuf, obuf, kc, kvall, cnt, qall, selfkv, num, numr, fin,
    s_kv, s_an, s_q, s_out, s_own,
    q_s, q_r, k_s, k_r, c_s, c_r, a_s, a_r, f_s, r_s, n_s, n_r, o_s, o_r,
):
    rows = ctx_q.shape[0]
    tile = pack.shape[2]
    tokens = tile // G
    planes = n // KVH
    span = KVH * tile
    me = lax.axis_index("hst")
    p = me // KVH
    m = me % KVH
    is_root = me == 0
    is_last = p == planes - 1
    low = m // 2 * 2
    far = (m + 2) % KVH

    def cols(g):
        return pl.ds(pl.multiple_of(g * DH, DH), DH)

    def wide(g):
        return pl.ds(pl.multiple_of(g * (G * DH), G * DH), G * DH)

    def load_kv(g, i, half, sem):
        src = (ctx_k, ctx_v)[i]
        return pltpu.make_async_copy(src.at[:, cols(g)], kc.at[g, i, half], sem.at[g, i])

    for g in range(KVH):
        for i in range(2):
            load_kv(g, i, 1, s_kv).start()

    @pl.when(is_root)
    def _():
        for g in range(KVH):
            for i in range(2):
                load_kv(g, i, 0, s_an).start()

    own_copies = [
        pltpu.make_async_copy(pack.at[m, 0], qall.at[me], s_own.at[0]),
        pltpu.make_async_copy(pack.at[0, 3], cnt.at[m], s_own.at[1]),
        pltpu.make_async_copy(ctx_k.at[:, cols(m)], kvall.at[m, 0], s_own.at[2]),
        pltpu.make_async_copy(ctx_v.at[:, cols(m)], kvall.at[m, 1], s_own.at[3]),
    ]
    own_self = pltpu.make_async_copy(pack.at[m, pl.ds(1, 2)], selfkv.at[me], s_own.at[4])
    q_loads = [
        pltpu.make_async_copy(ctx_q.at[:, wide(g)], qbuf.at[:, wide(g)], s_q.at[g])
        for g in range(KVH)
    ]
    for copy in own_copies:
        copy.start()

    @pl.when(is_last)
    def _():
        own_self.start()

    for copy in q_loads:
        copy.start()

    barrier = pltpu.get_barrier_semaphore()

    @pl.loop(1, n)
    def _(d):
        pl.semaphore_signal(
            barrier, inc=1, device_id={"hst": (me + d) % n}, device_id_type=pl.DeviceIdType.MESH
        )

    pl.semaphore_wait(barrier, n - 1)

    def q_send(d):
        target = (me + d) % n
        return remote(pack.at[target % KVH, 0], qall.at[me], q_s.at[d], q_r.at[me], target)

    @pl.loop(1, n)
    def _(d):
        q_send(d).start()

    def self_send(g):
        return remote(
            pack.at[g, pl.ds(1, 2)], selfkv.at[me], f_s.at[g], r_s.at[me], n - KVH + g
        )

    for g in range(KVH):
        @pl.when(me != n - KVH + g)
        def _():
            self_send(g).start()

    def cnt_send(d):
        g = (m + d) % KVH
        return remote(pack.at[0, 3], cnt.at[m], c_s.at[d], c_r.at[m], p * KVH + g)

    for d in range(1, KVH):
        cnt_send(d).start()

    for g in range(KVH):
        for i in range(2):
            load_kv(g, i, 1, s_kv).wait()

    def chunk_send(g, slot, target):
        piece = kc.at[g, :, 0]
        return remote(piece, piece, a_s.at[g, slot], a_r.at[g], target)

    def across(g):
        return chunk_send(g, 0, p * KVH + far)

    def beside(g):
        return chunk_send(g, 1, p * KVH + m + 1)

    def along(g, q):
        return chunk_send(g, 1 + q, q * KVH + m)

    even = m % 2 == 0
    first = [low, low + 1]
    second = [far // 2 * 2, far // 2 * 2 + 1]

    @pl.when(is_root)
    def _():
        for g in range(KVH):
            for i in range(2):
                load_kv(g, i, 0, s_an).wait()
        for g in (2, 3):
            across(g).start()
        for q in range(planes - 1, 0, -1):
            for g in (0, 1):
                along(g, q).start()

    def kv_send(d):
        g = (m + d) % KVH
        return remote(kc.at[g, :, 1], kvall.at[m], k_s.at[d], k_r.at[m], p * KVH + g)

    for d in (2, 3, 1):
        kv_send(d).start()

    @pl.when(is_root)
    def _():
        for g in (0, 1):
            across(g).start()
        for g in (0, 1, 2, 3):
            beside(g).start()

    def chunk_wait(g):
        chunk_send(g, 0, me).wait_recv()

    hub = (p == 0) & (m == 2)

    def take_first():
        @pl.when(jnp.logical_not(is_root))
        def _():
            for g in first:
                chunk_wait(g)

                @pl.when(hub)
                def _():
                    for q in range(planes - 1, 0, -1):
                        along(g, q).start()

                @pl.when(even & (p > 0))
                def _():
                    across(g).start()

                @pl.when(even)
                def _():
                    beside(g).start()

    def take_second():
        @pl.when(jnp.logical_not(is_root))
        def _():
            for g in second:
                chunk_wait(g)

                @pl.when(even)
                def _():
                    beside(g).start()

    early = hub | ((m == 0) & (p > 0))

    @pl.when(early)
    def _():
        take_first()

    @pl.loop(1, n)
    def _(d):
        source = (me + d) % n
        remote(pack.at[0, 0], qall.at[source], q_s.at[0], q_r.at[source], me).wait_recv()

    for copy in own_copies:
        copy.wait()

    for d in range(1, KVH):
        j = (m + d) % KVH
        remote(pack.at[0, 3], cnt.at[j], c_s.at[0], c_r.at[j], me).wait_recv()
        remote(kc.at[0, :, 1], kvall.at[j], k_s.at[0], k_r.at[j], me).wait_recv()

    def diagonal():
        return lax.broadcasted_iota(jnp.int32, (span, DH), 0) == lax.broadcasted_iota(
            jnp.int32, (span, DH), 1
        )

    def num_send(q):
        return remote(num.at[q], numr.at[p], n_s.at[q], n_r.at[p], q * KVH + m)

    def ask(with_self):
        lane = lax.broadcasted_iota(jnp.int32, (span, rows), 1).astype(jnp.float32)

        @pl.loop(0, planes)
        def _(step):
            q = (p + 1 + step) % planes
            queries = qall[pl.ds(q * KVH, KVH)].reshape(span, DH)
            best = total = summed = None
            for j in range(KVH):
                s = lax.dot_general(queries, kvall[j, 0], NT, preferred_element_type=jnp.float32)
                count = cnt[j].astype(jnp.float32)[0:1, :]
                s = jnp.where(lane < count, s, -jnp.inf)
                top = jnp.max(s, axis=1, keepdims=True)
                if with_self and j == KVH - 1:
                    keys = selfkv[:, 0].reshape(n * tile, DH)
                    values = selfkv[:, 1].reshape(n * tile, DH)
                    s2 = lax.dot_general(queries, keys, NT, preferred_element_type=jnp.float32)
                    shape = (span, n * tile)
                    at = lax.broadcasted_iota(jnp.int32, shape, 1)
                    row = lax.broadcasted_iota(jnp.int32, shape, 0)
                    shift = tile.bit_length() - 1
                    u = (at >> shift) * tokens + (at & (tile - 1))
                    t = (q * KVH + (row >> shift)) * tokens + (
                        (row & (tile - 1)) >> (G.bit_length() - 1)
                    )
                    s2 = jnp.where(((at & (tile - 1)) < tokens) & (u <= t), s2, -jnp.inf)
                    top = jnp.maximum(top, jnp.max(s2, axis=1, keepdims=True))
                e = jnp.exp2((s - top) * C)
                part = jnp.sum(e, axis=1, keepdims=True)
                mixed = lax.dot_general(
                    e.astype(jnp.bfloat16), kvall[j, 1], NN, preferred_element_type=jnp.float32
                )
                if with_self and j == KVH - 1:
                    e2 = jnp.exp2((s2 - top) * C)
                    part = part + jnp.sum(e2, axis=1, keepdims=True)
                    mixed = mixed + lax.dot_general(
                        e2.astype(jnp.bfloat16), values, NN, preferred_element_type=jnp.float32
                    )
                if best is None:
                    best, total, summed = top, part, mixed
                else:
                    peak = jnp.maximum(best, top)
                    old = jnp.exp2((best - peak) * C)
                    new = jnp.exp2((top - peak) * C)
                    best, total, summed = peak, total * old + part * new, summed * old + mixed * new
            num[q, pl.ds(0, span)] = summed
            diag = diagonal()
            line1 = jnp.sum(jnp.where(diag, best, 0.0), axis=0, keepdims=True)
            line2 = jnp.sum(jnp.where(diag, total, 0.0), axis=0, keepdims=True)
            pick = lax.broadcasted_iota(jnp.int32, (8, DH), 0) == 0
            num[q, pl.ds(span, 8)] = jnp.where(pick, line1, line2)

            @pl.when(q != p)
            def _():
                num_send(q).start()

    @pl.when(is_last)
    def _():
        own_self.wait()

        @pl.loop(1, n)
        def _(d):
            source = (me + d) % n
            remote(
                pack.at[0, pl.ds(1, 2)], selfkv.at[source], f_s.at[0], r_s.at[source], me
            ).wait_recv()

        ask(True)

    @pl.when(jnp.logical_not(is_last))
    def _():
        ask(False)

    def out_copy(g):
        return pltpu.make_async_copy(obuf.at[:, wide(g)], ctx_out.at[:, wide(g)], s_out.at[g])

    def context(g):
        pltpu.make_async_copy(ctx_q.at[:, wide(g)], qbuf.at[:, wide(g)], s_q.at[g]).wait()
        count = cnt[m].astype(jnp.float32)[0:1, :]
        row = lax.broadcasted_iota(jnp.int32, (rows, rows), 0)
        lane = lax.broadcasted_iota(jnp.int32, (rows, rows), 1)
        own = (lane <= row) & (lane.astype(jnp.float32) < count)
        outer = jnp.broadcast_to(me, (rows, rows)) > 0
        visible = jnp.concatenate([outer, own], axis=1)
        kept = lax.broadcasted_iota(jnp.int32, (rows, DH), 0).astype(jnp.float32) < count

        @pl.loop(0, G // 2)
        def _(pair):
            for k in range(2):
                at = pl.ds(pl.multiple_of((g * G + pair * 2 + k) * DH, DH), DH)
                keys = kc[g, 0].reshape(2 * rows, DH)
                values = kc[g, 1].reshape(2 * rows, DH)
                s = lax.dot_general(qbuf[:, at], keys, NT, preferred_element_type=jnp.float32)
                s = jnp.where(visible, s, -jnp.inf)
                top = jnp.max(s, axis=1, keepdims=True)
                e = jnp.exp2((s - top) * C)
                total = jnp.sum(e, axis=1, keepdims=True)
                mixed = lax.dot_general(
                    e.astype(jnp.bfloat16), values, NN, preferred_element_type=jnp.float32
                )
                out = jnp.where(kept, mixed * (1.0 / total), 0.0)
                obuf[:, at] = out.astype(jnp.bfloat16)

        out_copy(g).start()

    @pl.when(jnp.logical_not(early))
    def _():
        take_first()

    context(first[0])
    take_second()
    context(first[1])
    context(second[0])

    @pl.loop(1, planes)
    def _(d):
        q = (p + d) % planes
        remote(num.at[0], numr.at[q], n_s.at[0], n_r.at[q], me).wait_recv()

    def columns(block):
        diag = diagonal()
        best = jnp.sum(jnp.where(diag, block[0:1, :], 0.0), axis=1, keepdims=True)
        total = jnp.sum(jnp.where(diag, block[1:2, :], 0.0), axis=1, keepdims=True)
        return best, total

    best, total = columns(num[p, pl.ds(span, 8)])
    summed = num[p, pl.ds(0, span)]
    for d in range(1, planes):
        q = (p + d) % planes
        top, part = columns(numr[q, pl.ds(span, 8)])
        mixed = numr[q, pl.ds(0, span)]
        peak = jnp.maximum(best, top)
        old = jnp.exp2((best - peak) * C)
        new = jnp.exp2((top - peak) * C)
        best, total, summed = peak, total * old + part * new, summed * old + mixed * new
    fin[...] = (summed * (1.0 / total)).astype(jnp.bfloat16).reshape(KVH, tile, DH)

    def fin_send(d):
        j = (m + d) % KVH
        return remote(fin.at[j], ask_out.at[m], o_s.at[d], o_r.at[m], p * KVH + j)

    own_fin = pltpu.make_async_copy(fin.at[m], ask_out.at[m], s_own.at[5])
    for d in range(1, KVH):
        fin_send(d).start()
    own_fin.start()

    context(second[1])

    own_fin.wait()
    for d in range(1, KVH):
        j = (m + d) % KVH
        remote(fin.at[0], ask_out.at[j], o_s.at[0], o_r.at[j], me).wait_recv()
        fin_send(d).wait_send()
        cnt_send(d).wait_send()
        kv_send(d).wait_send()
    for g in range(KVH):
        out_copy(g).wait()

        @pl.when(me != n - KVH + g)
        def _():
            self_send(g).wait_send()

    @pl.loop(1, n)
    def _(d):
        q_send(d).wait_send()

    @pl.loop(1, planes)
    def _(d):
        num_send((p + d) % planes).wait_send()

    @pl.when(is_root)
    def _():
        for g in range(KVH):
            across(g).wait_send()
            beside(g).wait_send()
        for q in range(1, planes):
            for g in (0, 1):
                along(g, q).wait_send()

    @pl.when(even & jnp.logical_not(is_root))
    def _():
        for g in first + second:
            beside(g).wait_send()

        @pl.when(p > 0)
        def _():
            for g in first:
                across(g).wait_send()

    @pl.when(hub)
    def _():
        for g in first:
            for q in range(1, planes):
                along(g, q).wait_send()


def body(n, ctx_q, ctx_k, ctx_v, ask_q, ask_k, ask_v, valid):
    rows = ctx_q.shape[0]
    tokens = ask_q.shape[0]
    tile = tokens * G
    planes = n // KVH
    span = KVH * tile

    def heads(x):
        x = x.reshape(tokens, KVH, -1, DH).transpose(1, 0, 2, 3).reshape(KVH, -1, DH)
        return jnp.pad(x, ((0, 0), (0, tile - x.shape[1]), (0, 0)))

    count = jnp.broadcast_to(valid.astype(jnp.bfloat16).reshape(1, 1, 1), (KVH, tile, DH))
    pack = jnp.stack([heads(ask_q), heads(ask_k), heads(ask_v), count], axis=1)
    dma = pltpu.SemaphoreType.DMA
    bf = jnp.bfloat16
    ctx_out, ask_out = pl.pallas_call(
        functools.partial(kernel, n),
        out_shape=(
            jax.ShapeDtypeStruct(ctx_q.shape, bf),
            jax.ShapeDtypeStruct((KVH, tile, DH), bf),
        ),
        in_specs=[pl.BlockSpec(memory_space=pl.ANY)] * 4,
        out_specs=(pl.BlockSpec(memory_space=pl.ANY),) * 2,
        scratch_shapes=[
            pltpu.VMEM(ctx_q.shape, bf),
            pltpu.VMEM(ctx_q.shape, bf),
            pltpu.VMEM((KVH, 2, 2, rows, DH), bf),
            pltpu.VMEM((KVH, 2, rows, DH), bf),
            pltpu.VMEM((KVH, tile, DH), bf),
            pltpu.VMEM((n, tile, DH), bf),
            pltpu.VMEM((n, 2, tile, DH), bf),
            pltpu.VMEM((planes, span + 8, DH), jnp.float32),
            pltpu.VMEM((planes, span + 8, DH), jnp.float32),
            pltpu.VMEM((KVH, tile, DH), bf),
            dma((KVH, 2)),
            dma((KVH, 2)),
            dma((KVH,)),
            dma((KVH,)),
            dma((6,)),
            dma((n,)),
            dma((n,)),
            dma((KVH,)),
            dma((KVH,)),
            dma((KVH,)),
            dma((KVH,)),
            dma((KVH, planes + 1)),
            dma((KVH,)),
            dma((KVH,)),
            dma((n,)),
            dma((planes,)),
            dma((planes,)),
            dma((KVH,)),
            dma((KVH,)),
        ],
        compiler_params=pltpu.CompilerParams(collective_id=0, has_side_effects=True),
    )(ctx_q, ctx_k, ctx_v, pack)
    ask_out = ask_out.reshape(KVH, tokens, G, DH).transpose(1, 0, 2, 3).reshape(tokens, H * DH)
    return ctx_out, ask_out


def solution(mesh):
    n = mesh.shape["hst"]
    rows = P(("req", "hst"), None)
    return jax.shard_map(
        functools.partial(body, n),
        mesh=mesh,
        in_specs=(rows,) * 6 + (P(("req", "hst")),),
        out_specs=(rows, rows),
        check_vma=False,
    )
```

time: 222 us -> 38.1 us (0.17); the launches traced: 218 us -> 37.7 us
  waiting for transfers between devices: 85.5 us -> 0 us
  blocking collectives: 57.1 us -> 0 us
  Pallas kernels: 0 us -> 31.3 us
  local copies, waits for them, and re-layouts: 27.2 us -> 4.47 us
  starting transfers between devices: 16.3 us -> 0 us
  between operations: 14.9 us -> 1.3 us
  other arithmetic: 11.6 us -> 0.71 us
  matrix products: 5.35 us -> 0 us
    psum x1 -> x0, waiting for transfers between devices: 77.9 us -> none  [from_root(): return lax.psum(jnp.where(mine, array, jnp.zeros_like(array)), axis)]
    all_gather x3 -> x0, blocking collectives: 57.1 us -> none  [the longest x1 20.3 us: body(): lax.all_gather(ask_q, 'hst', axis=0, tiled=True)]
    pallas_call x0 -> x1, Pallas kernels: none -> 31.3 us  [body(): pl.pallas_call(functools.partial(kernel, n), out_shape=(jax.ShapeDtypeStr...]
    all_to_all x3 -> x0, starting transfers between devices: 16.2 us -> none  [the longest x1 6.36 us: body(): lax.all_to_all(ask_max[None], 'hst', split_axis=1, concat_axis=0, tiled=T...]
    dynamic_update_slice x24 -> x0, local copies, waits for them, and re-layouts: 15.5 us -> none  [the longest x8 5.62 us: one_group(): lax.dynamic_update_slice_in_dim(totals, row_sum, group_index * group_size...]
    all_to_all x3 -> x0, waiting for transfers between devices: 7.66 us -> none  [the longest x1 4.02 us: body(): lax.all_to_all(ask_max[None], 'hst', split_axis=1, concat_axis=0, tiled=T...]
    dot_general x16 -> x0, matrix products: 5.35 us -> none  [the longest x8 2.9 us: one_group(): jnp.einsum('rgd,sd->rgs', query_part, key_part, preferred_element_type=jn...]
    dynamic_slice x8 -> x0, local copies, waits for them, and re-layouts: 4.54 us -> none  [one_group(): lax.dynamic_slice_in_dim(queries, group_index * group_width, group_width, 1)]
  transfers between devices with their start and end apart: 4 -> 0, of which waited for: 3 -> 0; matrix products, arithmetic and copies ran while one was open for 11% -> 0% of each run, Pallas kernels for 0% -> 0%
where the time goes in v1:
time: 38.1 us; the launch traced here: 37.7 us
  Pallas kernels  31.3 us (82%)
  local copies, waits for them, and re-layouts  4.47 us (12%)
  between operations  1.3 us (3%)
  other arithmetic  0.71 us (2%)
    pallas_call x1, Pallas kernels, body(): pl.pallas_call(functools.partial(kernel, n), out_shape=(jax.ShapeDtypeStr...  31.3 us
    unnamed x7, local copies, waits for them, and re-layouts  3.63 us
    another operation x3, local copies, waits for them, and re-layouts, body(): pack = jnp.stack([heads(ask_q), heads(ask_k), heads(ask_v), count], axis=1)  0.83 us

profile of v1, /device:TPU:9, one launch (start us, length us, event | category | flops | bytes accessed | tf_op | source)
XLA Modules:
  0.0 37.7 jit_solution(13436386646232036464)
XLA Ops:
  1.3 0.1 pad.12.clone
  1.4 0.0 copy-start
  1.4 0.0 copy-start.1
  1.4 0.7 %copy_bitcast_fusion.3 = bf16[4,1,16,128]{3,2,1,0:T(8,128)(2,1)S(1)} fusion(bf16[1,2,32,128]{3,1,2,0:T(2,128)(2,1)} %bitcast.35), kind=kLoop, calls=%fused_computation.4 | loop fusion | bytes 32768 | tf_op jit(solution)/shard_map/stack | solution.py:441
  2.1 0.0 copy-done
  2.1 0.0 copy-done.1
  2.1 0.7 %maximum_maximum_fusion.pack = bf16[4,4,16,128]{3,2,1,0:T(8,128)(2,1)} fusion(bf16[4,1,16,128]{3,2,1,0:T(8,128)(2,1)S(1)} %get-tuple-element.6, bf16[4,1,16,128]{3,2,1,0:T(8,128)(2,1)S(1)} %get-tuple-element.7, bf16[4,1,16,128]{3,2,1,0:T(8,128)(2,1)S(1)} %copy_bitcast_fusion.3, bf16[4]{0:T(256)(128)(2,1)S(1)} %pad.12.clone), kind=kLoop, calls=%fused_computation | loop fusion | flops 98304 | bytes 114696 | tf_op jit(solution)/shard_map/stack | solution.py:441
  2.8 31.3 %shard_map.86 = (bf16[128,4096]{1,0:T(8,128)(2,1)}, bf16[4,16,128]{2,1,0:T(8,128)(2,1)}) custom-call(bf16[128,4096]{1,0:T(8,128)(2,1)} %ctx_q.1, bf16[128,512]{1,0:T(8,128)(2,1)} %ctx_k.1, bf16[128,512]{1,0:T(8,128)(2,1)} %ctx_v.1, bf16[4,4,16,128]{3,2,1,0:T(8,128)(2,1)} %maximum_maximum_fusion.pack), custom_call_target="tpu_custom_call" | custom-call | tf_op jit(solution)/shard_map/pallas_call | solution.py:444
  34.1 0.7 %copy_bitcast_fusion.2 = bf16[1,2,32,128]{3,2,1,0:T(8,128)(2,1)S(1)} fusion(bf16[4,16,128]{2,1,0:T(8,128)(2,1)} %get-tuple-element.5), kind=kLoop, calls=%fused_computation.3 | loop fusion | bytes 32768
  34.8 0.6 %copy.18 = bf16[1,2,32,128]{3,1,2,0:T(2,128)(2,1)} copy(bf16[1,2,32,128]{3,2,1,0:T(8,128)(2,1)S(1)} %copy_bitcast_fusion.2) | data formatting | bytes 32768
  35.5 2.3 %copy.21 = bf16[128,4096]{1,0:T(8,128)(2,1)} copy(bf16[128,4096]{1,0:T(8,128)(2,1)} %get-tuple-element.10) | data formatting | bytes 2097152
  (1 shorter events, 0.0 us)
Async XLA Ops:
  1.4 0.8 %copy-start = (bf16[2,512]{1,0:T(2,128)(2,1)S(1)}, bf16[2,512]{1,0:T(2,128)(2,1)}, u32[]{:S(2)}) copy-start(bf16[2,512]{1,0:T(2,128)(2,1)} %param.12) | copy-start | bytes 6148
  1.4 0.8 %copy-start.1 = (bf16[2,512]{1,0:T(2,128)(2,1)S(1)}, bf16[2,512]{1,0:T(2,128)(2,1)}, u32[]{:S(2)}) copy-start(bf16[2,512]{1,0:T(2,128)(2,1)} %param.11) | copy-start | bytes 6148

commit v2 on v1

--- a/solution.py
+++ b/solution.py
@@ -12,6 +12,8 @@
 KVH = 4
 DH = 128
 G = H // KVH
+UNROLL = 8
+PAIR = 2
 C = math.log2(math.e) / math.sqrt(DH)
 NT = (((1,), (1,)), ((), ()))
 NN = (((1,), (0,)), ((), ()))
@@ -231,60 +233,65 @@
         return remote(num.at[q], numr.at[p], n_s.at[q], n_r.at[p], q * KVH + m)
 
     def ask(with_self):
-        lane = lax.broadcasted_iota(jnp.int32, (span, rows), 1).astype(jnp.float32)
-
-        @pl.loop(0, planes)
+        total_rows = PAIR * span
+        lane = lax.broadcasted_iota(jnp.int32, (total_rows, rows), 1).astype(jnp.float32)
+
+        @pl.loop(0, planes // PAIR)
         def _(step):
-            q = (p + 1 + step) % planes
-            queries = qall[pl.ds(q * KVH, KVH)].reshape(span, DH)
-            best = total = summed = None
-            for j in range(KVH):
-                s = lax.dot_general(queries, kvall[j, 0], NT, preferred_element_type=jnp.float32)
-                count = cnt[j].astype(jnp.float32)[0:1, :]
-                s = jnp.where(lane < count, s, -jnp.inf)
-                top = jnp.max(s, axis=1, keepdims=True)
-                if with_self and j == KVH - 1:
-                    keys = selfkv[:, 0].reshape(n * tile, DH)
-                    values = selfkv[:, 1].reshape(n * tile, DH)
-                    s2 = lax.dot_general(queries, keys, NT, preferred_element_type=jnp.float32)
-                    shape = (span, n * tile)
-                    at = lax.broadcasted_iota(jnp.int32, shape, 1)
-                    row = lax.broadcasted_iota(jnp.int32, shape, 0)
-                    shift = tile.bit_length() - 1
-                    u = (at >> shift) * tokens + (at & (tile - 1))
-                    t = (q * KVH + (row >> shift)) * tokens + (
-                        (row & (tile - 1)) >> (G.bit_length() - 1)
-                    )
-                    s2 = jnp.where(((at & (tile - 1)) < tokens) & (u <= t), s2, -jnp.inf)
-                    top = jnp.maximum(top, jnp.max(s2, axis=1, keepdims=True))
-                e = jnp.exp2((s - top) * C)
-                part = jnp.sum(e, axis=1, keepdims=True)
-                mixed = lax.dot_general(
-                    e.astype(jnp.bfloat16), kvall[j, 1], NN, preferred_element_type=jnp.float32
+            at_planes = [(p + 1 + step * PAIR + k) % planes for k in range(PAIR)]
+            queries = jnp.concatenate(
+                [qall[pl.ds(q * KVH, KVH)].reshape(span, DH) for q in at_planes], axis=0
+            )
+            s = [
+                lax.dot_general(queries, kvall[j, 0], NT, preferred_element_type=jnp.float32)
+                for j in range(KVH)
+            ]
+            s = [
+                jnp.where(lane < cnt[j].astype(jnp.float32)[0:1, :], s[j], -jnp.inf)
+                for j in range(KVH)
+            ]
+            values = [kvall[j, 1] for j in range(KVH)]
+            top = [jnp.max(x, axis=1, keepdims=True) for x in s]
+            if with_self:
+                keys = selfkv[:, 0].reshape(n * tile, DH)
+                s2 = lax.dot_general(queries, keys, NT, preferred_element_type=jnp.float32)
+                shape = (total_rows, n * tile)
+                at = lax.broadcasted_iota(jnp.int32, shape, 1)
+                row = lax.broadcasted_iota(jnp.int32, shape, 0)
+                base = jnp.where(row < span, at_planes[0] * span, at_planes[-1] * span - span)
+                shift = tile.bit_length() - 1
+                u = (at >> shift) * tokens + (at & (tile - 1))
+                t = (base + row) >> (G.bit_length() - 1)
+                s2 = jnp.where(((at & (tile - 1)) < tokens) & (u <= t), s2, -jnp.inf)
+                s[-1] = jnp.concatenate([s[-1], s2], axis=1)
+                values[-1] = jnp.concatenate(
+                    [values[-1], selfkv[:, 1].reshape(n * tile, DH)], axis=0
                 )
-                if with_self and j == KVH - 1:
-                    e2 = jnp.exp2((s2 - top) * C)
-                    part = part + jnp.sum(e2, axis=1, keepdims=True)
-                    mixed = mixed + lax.dot_general(
-                        e2.astype(jnp.bfloat16), values, NN, preferred_element_type=jnp.float32
-                    )
-                if best is None:
-                    best, total, summed = top, part, mixed
-                else:
-                    peak = jnp.maximum(best, top)
-                    old = jnp.exp2((best - peak) * C)
-                    new = jnp.exp2((top - peak) * C)
-                    best, total, summed = peak, total * old + part * new, summed * old + mixed * new
-            num[q, pl.ds(0, span)] = summed
+                top[-1] = jnp.maximum(top[-1], jnp.max(s2, axis=1, keepdims=True))
+            e = [jnp.exp2((x - y) * C) for x, y in zip(s, top)]
+            part = [jnp.sum(x, axis=1, keepdims=True) for x in e]
+            mixed = [
+                lax.dot_general(
+                    x.astype(jnp.bfloat16), v, NN, preferred_element_type=jnp.float32
+                )
+                for x, v in zip(e, values)
+            ]
+            best = functools.reduce(jnp.maximum, top)
+            factor = [jnp.exp2((x - best) * C) for x in top]
+            total = sum(x * y for x, y in zip(part, factor))
+            summed = sum(x * y for x, y in zip(mixed, factor))
             diag = diagonal()
-            line1 = jnp.sum(jnp.where(diag, best, 0.0), axis=0, keepdims=True)
-            line2 = jnp.sum(jnp.where(diag, total, 0.0), axis=0, keepdims=True)
             pick = lax.broadcasted_iota(jnp.int32, (8, DH), 0) == 0
-            num[q, pl.ds(span, 8)] = jnp.where(pick, line1, line2)
-
-            @pl.when(q != p)
-            def _():
-                num_send(q).start()
+            for k, q in enumerate(at_planes):
+                cut = slice(k * span, (k + 1) * span)
+                num[q, pl.ds(0, span)] = summed[cut]
+                line1 = jnp.sum(jnp.where(diag, best[cut], 0.0), axis=0, keepdims=True)
+                line2 = jnp.sum(jnp.where(diag, total[cut], 0.0), axis=0, keepdims=True)
+                num[q, pl.ds(span, 8)] = jnp.where(pick, line1, line2)
+            for q in at_planes:
+                @pl.when(q != p)
+                def _():
+                    num_send(q).start()
 
     @pl.when(is_last)
     def _():
@@ -316,22 +323,31 @@
         visible = jnp.concatenate([outer, own], axis=1)
         kept = lax.broadcasted_iota(jnp.int32, (rows, DH), 0).astype(jnp.float32) < count
 
-        @pl.loop(0, G // 2)
-        def _(pair):
-            for k in range(2):
-                at = pl.ds(pl.multiple_of((g * G + pair * 2 + k) * DH, DH), DH)
-                keys = kc[g, 0].reshape(2 * rows, DH)
-                values = kc[g, 1].reshape(2 * rows, DH)
-                s = lax.dot_general(qbuf[:, at], keys, NT, preferred_element_type=jnp.float32)
-                s = jnp.where(visible, s, -jnp.inf)
-                top = jnp.max(s, axis=1, keepdims=True)
-                e = jnp.exp2((s - top) * C)
-                total = jnp.sum(e, axis=1, keepdims=True)
-                mixed = lax.dot_general(
-                    e.astype(jnp.bfloat16), values, NN, preferred_element_type=jnp.float32
+        @pl.loop(0, G // UNROLL)
+        def _(step):
+            keys = kc[g, 0].reshape(2 * rows, DH)
+            values = kc[g, 1].reshape(2 * rows, DH)
+            at = [
+                pl.ds(pl.multiple_of((g * G + step * UNROLL + k) * DH, DH), DH)
+                for k in range(UNROLL)
+            ]
+            s = [
+                lax.dot_general(qbuf[:, x], keys, NT, preferred_element_type=jnp.float32)
+                for x in at
+            ]
+            s = [jnp.where(visible, x, -jnp.inf) for x in s]
+            top = [jnp.max(x, axis=1, keepdims=True) for x in s]
+            e = [jnp.exp2((x - y) * C) for x, y in zip(s, top)]
+            total = [jnp.sum(x, axis=1, keepdims=True) for x in e]
+            mixed = [
+                lax.dot_general(
+                    x.astype(jnp.bfloat16), values, NN, preferred_element_type=jnp.float32
                 )
-                out = jnp.where(kept, mixed * (1.0 / total), 0.0)
-                obuf[:, at] = out.astype(jnp.bfloat16)
+                for x in e
+            ]
+            for k in range(UNROLL):
+                out = jnp.where(kept, mixed[k] * (1.0 / total[k]), 0.0)
+                obuf[:, at[k]] = out.astype(jnp.bfloat16)
 
         out_copy(g).start()
 

time: 38.1 us -> 32.9 us (0.86)
  the two profiles are of different devices: /device:TPU:9 before, /device:TPU:13 now
where the time goes in v2:
time: 32.9 us; the launch traced here: 32.5 us
  Pallas kernels  26.1 us (79%)
  local copies, waits for them, and re-layouts  4.47 us (14%)
  between operations  1.3 us (4%)
  other arithmetic  0.71 us (2%)
    pallas_call x1, Pallas kernels, body(): pl.pallas_call(functools.partial(kernel, n), out_shape=(jax.ShapeDtypeStr...  26.1 us
    unnamed x7, local copies, waits for them, and re-layouts  3.63 us
    another operation x3, local copies, waits for them, and re-layouts, body(): pack = jnp.stack([heads(ask_q), heads(ask_k), heads(ask_v), count], axis=1)  0.83 us
    another operation x1, other arithmetic, body(): pack = jnp.stack([heads(ask_q), heads(ask_k), heads(ask_v), count], axis=1)  0.71 us

profile of v2, /device:TPU:13, one launch (start us, length us, event | category | flops | bytes accessed | tf_op | source)
XLA Modules:
  0.0 32.5 jit_solution(4113057690613025380)
XLA Ops:
  1.3 0.1 pad.12.clone
  1.4 0.0 copy-start
  1.4 0.0 copy-start.1
  1.4 0.7 %copy_bitcast_fusion.3 = bf16[4,1,16,128]{3,2,1,0:T(8,128)(2,1)S(1)} fusion(bf16[1,2,32,128]{3,1,2,0:T(2,128)(2,1)} %bitcast.35), kind=kLoop, calls=%fused_computation.4 | loop fusion | bytes 32768 | tf_op jit(solution)/shard_map/stack | solution.py:457
  2.1 0.0 copy-done
  2.1 0.0 copy-done.1
  2.1 0.7 %maximum_maximum_fusion.pack = bf16[4,4,16,128]{3,2,1,0:T(8,128)(2,1)} fusion(bf16[4,1,16,128]{3,2,1,0:T(8,128)(2,1)S(1)} %get-tuple-element.6, bf16[4,1,16,128]{3,2,1,0:T(8,128)(2,1)S(1)} %get-tuple-element.7, bf16[4,1,16,128]{3,2,1,0:T(8,128)(2,1)S(1)} %copy_bitcast_fusion.3, bf16[4]{0:T(256)(128)(2,1)S(1)} %pad.12.clone), kind=kLoop, calls=%fused_computation | loop fusion | flops 98304 | bytes 114696 | tf_op jit(solution)/shard_map/stack | solution.py:457
  2.8 26.1 %shard_map.86 = (bf16[128,4096]{1,0:T(8,128)(2,1)}, bf16[4,16,128]{2,1,0:T(8,128)(2,1)}) custom-call(bf16[128,4096]{1,0:T(8,128)(2,1)} %ctx_q.1, bf16[128,512]{1,0:T(8,128)(2,1)} %ctx_k.1, bf16[128,512]{1,0:T(8,128)(2,1)} %ctx_v.1, bf16[4,4,16,128]{3,2,1,0:T(8,128)(2,1)} %maximum_maximum_fusion.pack), custom_call_target="tpu_custom_call" | custom-call | tf_op jit(solution)/shard_map/pallas_call | solution.py:460
  28.9 0.7 %copy_bitcast_fusion.2 = bf16[1,2,32,128]{3,2,1,0:T(8,128)(2,1)S(1)} fusion(bf16[4,16,128]{2,1,0:T(8,128)(2,1)} %get-tuple-element.5), kind=kLoop, calls=%fused_computation.3 | loop fusion | bytes 32768
  29.6 0.6 %copy.18 = bf16[1,2,32,128]{3,1,2,0:T(2,128)(2,1)} copy(bf16[1,2,32,128]{3,2,1,0:T(8,128)(2,1)S(1)} %copy_bitcast_fusion.2) | data formatting | bytes 32768
  30.2 2.3 %copy.21 = bf16[128,4096]{1,0:T(8,128)(2,1)} copy(bf16[128,4096]{1,0:T(8,128)(2,1)} %get-tuple-element.10) | data formatting | bytes 2097152
  (1 shorter events, 0.0 us)
Async XLA Ops:
  1.4 0.8 %copy-start = (bf16[2,512]{1,0:T(2,128)(2,1)S(1)}, bf16[2,512]{1,0:T(2,128)(2,1)}, u32[]{:S(2)}) copy-start(bf16[2,512]{1,0:T(2,128)(2,1)} %param.12) | copy-start | bytes 6148
  1.4 0.8 %copy-start.1 = (bf16[2,512]{1,0:T(2,128)(2,1)S(1)}, bf16[2,512]{1,0:T(2,128)(2,1)}, u32[]{:S(2)}) copy-start(bf16[2,512]{1,0:T(2,128)(2,1)} %param.11) | copy-start | bytes 6148

commit v3 on v2

--- a/solution.py
+++ b/solution.py
@@ -358,7 +358,6 @@
     context(first[0])
     take_second()
     context(first[1])
-    context(second[0])
 
     @pl.loop(1, planes)
     def _(d):
@@ -392,6 +391,7 @@
         fin_send(d).start()
     own_fin.start()
 
+    context(second[0])
     context(second[1])
 
     own_fin.wait()

time: 32.9 us -> 32.5 us (0.988)
  the two profiles are of different devices: /device:TPU:13 before, /device:TPU:9 now
where the time goes in v3:
time: 32.5 us; the launch traced here: 32.1 us
  Pallas kernels  25.7 us (79%)
  local copies, waits for them, and re-layouts  4.47 us (14%)
  between operations  1.3 us (4%)
  other arithmetic  0.71 us (2%)
    pallas_call x1, Pallas kernels, body(): pl.pallas_call(functools.partial(kernel, n), out_shape=(jax.ShapeDtypeStr...  25.7 us
    unnamed x7, local copies, waits for them, and re-layouts  3.63 us
    another operation x3, local copies, waits for them, and re-layouts, body(): pack = jnp.stack([heads(ask_q), heads(ask_k), heads(ask_v), count], axis=1)  0.83 us
    another operation x1, other arithmetic, body(): pack = jnp.stack([heads(ask_q), heads(ask_k), heads(ask_v), count], axis=1)  0.71 us

profile of v3, /device:TPU:9, one launch (start us, length us, event | category | flops | bytes accessed | tf_op | source)
XLA Modules:
  0.0 32.1 jit_solution(6139799639344920345)
XLA Ops:
  1.3 0.1 pad.12.clone
  1.4 0.0 copy-start
  1.4 0.0 copy-start.1
  1.4 0.7 %copy_bitcast_fusion.3 = bf16[4,1,16,128]{3,2,1,0:T(8,128)(2,1)S(1)} fusion(bf16[1,2,32,128]{3,1,2,0:T(2,128)(2,1)} %bitcast.35), kind=kLoop, calls=%fused_computation.4 | loop fusion | bytes 32768 | tf_op jit(solution)/shard_map/stack | solution.py:457
  2.1 0.0 copy-done
  2.1 0.0 copy-done.1
  2.1 0.7 %maximum_maximum_fusion.pack = bf16[4,4,16,128]{3,2,1,0:T(8,128)(2,1)} fusion(bf16[4,1,16,128]{3,2,1,0:T(8,128)(2,1)S(1)} %get-tuple-element.6, bf16[4,1,16,128]{3,2,1,0:T(8,128)(2,1)S(1)} %get-tuple-element.7, bf16[4,1,16,128]{3,2,1,0:T(8,128)(2,1)S(1)} %copy_bitcast_fusion.3, bf16[4]{0:T(256)(128)(2,1)S(1)} %pad.12.clone), kind=kLoop, calls=%fused_computation | loop fusion | flops 98304 | bytes 114696 | tf_op jit(solution)/shard_map/stack | solution.py:457
  2.8 25.7 %shard_map.86 = (bf16[128,4096]{1,0:T(8,128)(2,1)}, bf16[4,16,128]{2,1,0:T(8,128)(2,1)}) custom-call(bf16[128,4096]{1,0:T(8,128)(2,1)} %ctx_q.1, bf16[128,512]{1,0:T(8,128)(2,1)} %ctx_k.1, bf16[128,512]{1,0:T(8,128)(2,1)} %ctx_v.1, bf16[4,4,16,128]{3,2,1,0:T(8,128)(2,1)} %maximum_maximum_fusion.pack), custom_call_target="tpu_custom_call" | custom-call | tf_op jit(solution)/shard_map/pallas_call | solution.py:460
  28.5 0.7 %copy_bitcast_fusion.2 = bf16[1,2,32,128]{3,2,1,0:T(8,128)(2,1)S(1)} fusion(bf16[4,16,128]{2,1,0:T(8,128)(2,1)} %get-tuple-element.5), kind=kLoop, calls=%fused_computation.3 | loop fusion | bytes 32768
  29.2 0.6 %copy.18 = bf16[1,2,32,128]{3,1,2,0:T(2,128)(2,1)} copy(bf16[1,2,32,128]{3,2,1,0:T(8,128)(2,1)S(1)} %copy_bitcast_fusion.2) | data formatting | bytes 32768
  29.9 2.3 %copy.21 = bf16[128,4096]{1,0:T(8,128)(2,1)} copy(bf16[128,4096]{1,0:T(8,128)(2,1)} %get-tuple-element.10) | data formatting | bytes 2097152
  (1 shorter events, 0.0 us)
Async XLA Ops:
  1.4 0.8 %copy-start = (bf16[2,512]{1,0:T(2,128)(2,1)S(1)}, bf16[2,512]{1,0:T(2,128)(2,1)}, u32[]{:S(2)}) copy-start(bf16[2,512]{1,0:T(2,128)(2,1)} %param.12) | copy-start | bytes 6148
  1.4 0.8 %copy-start.1 = (bf16[2,512]{1,0:T(2,128)(2,1)S(1)}, bf16[2,512]{1,0:T(2,128)(2,1)}, u32[]{:S(2)}) copy-start(bf16[2,512]{1,0:T(2,128)(2,1)} %param.11) | copy-start | bytes 6148
